TPU v7x, 128 devices: a whole 4x4x4 slice. The times are simulated.
128 devices in a mesh: row: 8 (over z, core), col: 16 (over y, x).
Axes of the slice: x: 4, y: 4, z: 4, core: 2. Of those that a mesh axis runs over, the one named last changes fastest.
Arguments:
- wrf_forcing: float32 [7, 128, 256], P(None, ('row', 'col')), may hold values from 0 to 1
- ground_height_km: float32 [2048, 4096], P('row', 'col'), may hold values from 0.2 to 3
- reflected_share: float32 [2048, 4096], P('row', 'col'), may hold values from 0.35 to 0.85
- snow_water: float32 [2048, 4096], P('row', 'col'), may hold values from 0 to 6
- soil_water: float32 [2048, 4096], P('row', 'col'), may hold values from 1 to 8
- saturated: float32 [2048, 4096], P('row', 'col'), may hold values from 0.5 to 4
- release_rate: float32 [2048, 4096], P('row', 'col'), may hold values from 0.05 to 0.3
- mfd_weights: bfloat16 [8, 2048, 4096], P(None, 'row', 'col'), may hold values from 0 to 1, as said below
- cell_segment: int32 [2048, 4096], P('row', 'col'), may hold values from 0 to 127
- route_inverse: float32 [128, 2048, 128], P('row', 'col'), may hold values from 0 to 1, as said below
- transfer: float32 [128, 2048], P('row', 'col'), may hold values from 0.96 to 1
- downstream: int32 [128, 16], P('row', 'col'), may hold values from 1 to 16, as said below
Outputs:
- snowpack: float32 [2048, 4096], P('row', 'col')
- soil_moisture: float32 [2048, 4096], P('row', 'col')
- groundwater: float32 [2048, 4096], P('row', 'col')
- channel_flow: float32 [128, 2048], P('row', 'col')
Inputs may be any that keep to these rules, and one draw needn't show every extreme that they name: `mfd_weights`: the eight shares of a cell are positive and add up to less than one. `route_inverse`: entries are positive and every column of each block's 128 by 128 matrix sums to one. `downstream`: block b of a device drains into block b + 1, b + 2 or b + 3 of the same device and column group, and 16 means the flow leaves toward the next column group.
All inputs are finite; a program needn't handle non-finite values.
Results may differ from a plain program's by a relative error of at most 0.0005.
Values may be sent and summed in bfloat16 or wider, within the bound.
A program may use at most 64 MiB of HBM per device.

v0:
```python
import jax
import jax.numpy as jnp
from jax import lax
from jax.sharding import PartitionSpec as P

FAC = 16
SEG = 128
SWEEPS = 8


OFFSETS = ((-1, -1), (-1, 0), (-1, 1), (0, -1), (0, 1), (1, -1), (1, 0), (1, 1))
precise = lax.Precision.HIGHEST


def for_sending(value):
    return jax.tree.map(lambda a: a.astype(jnp.bfloat16) if a.dtype == jnp.float32 else a, value)


def padded_2(cells, sides, width):
    for axis, dim in sides:
        count = lax.axis_size(axis)
        ends = count - 1
        head = lax.slice_in_dim(cells, 0, width, axis=dim)
        tail = lax.slice_in_dim(cells, cells.shape[dim] - width, cells.shape[dim], axis=dim)
        cells = jnp.concatenate(
            [
                lax.ppermute(tail, axis, [(i, (i + 1) % count) for i in range(ends)]),
                cells,
                lax.ppermute(head, axis, [((i + 1) % count, i) for i in range(ends)]),
            ],
            axis=dim,
        )
    return cells


def passed_along(value, axis, by):
    peers = lax.axis_size(axis)
    pairs = [(i, i + by) for i in range(peers) if 0 <= i + by < peers]
    return lax.ppermute(value, axis, pairs)


def interp_matrix(cell_count, coarse):
    cell_index = jnp.arange(cell_count, dtype=jnp.int32)
    numerator = 2 * cell_index + 1 - FAC
    lower_point = numerator // (2 * FAC)
    fraction = (numerator - 2 * FAC * lower_point).astype(jnp.float32) / (2.0 * FAC)
    column = jnp.arange(coarse + 2, dtype=jnp.int32)
    first_weight = (column[None, :] == (lower_point + 1)[:, None]).astype(jnp.float32)
    second = (column[None, :] == (lower_point + 2)[:, None]).astype(jnp.float32)
    return first_weight * (1.0 - fraction)[:, None] + second * fraction[:, None]


def downscale(padded, row_matrix, col_matrix):
    rows_done = jnp.einsum("ik,vkl->vil", row_matrix, padded, precision=precise)
    return jnp.einsum("vil,jl->vij", rows_done, col_matrix, precision=precise)


def extend_rows(padded):
    at_top = lax.axis_index("row") == 0
    at_bottom = lax.axis_index("row") == lax.axis_size("row") - 1
    padded = padded.at[:, 0, :].set(jnp.where(at_top, padded[:, 1, :], padded[:, 0, :]))
    padded = padded.at[:, -1, :].set(jnp.where(at_bottom, padded[:, -2, :], padded[:, -1, :]))
    return padded


def energy_balance(
    meteorological_drivers, ground_height_km, reflected_share, snow_water, soil_water, saturated
):
    lowlevel_heat_degree = (
        -10.0
        + 20.0 * meteorological_drivers[0]
        + 6.5 * (0.5 + 2.0 * meteorological_drivers[6] - ground_height_km)
    )
    solar_incoming_flux = 0.8 * meteorological_drivers[1]
    thermal_infrared_flux = 0.25 + 0.15 * meteorological_drivers[2]
    deficit = 1.5 * meteorological_drivers[3]
    lowlevel_breeze_rate = 0.5 + 6.0 * meteorological_drivers[4]
    overall_rain_depth = 4.0 * meteorological_drivers[5]
    frozen_fall_depth = overall_rain_depth / (1.0 + jnp.exp(lowlevel_heat_degree / 1.5))
    rainfall = overall_rain_depth - frozen_fall_depth
    heat_gain_budget = (
        solar_incoming_flux * (1.0 - reflected_share)
        + thermal_infrared_flux
        - 0.3
        + 0.02 * lowlevel_breeze_rate * lowlevel_heat_degree
    )
    melted = jnp.minimum(10.8 * jnp.maximum(heat_gain_budget, 0.0), snow_water + frozen_fall_depth)
    snowpack = snow_water + frozen_fall_depth - melted
    wetted = soil_water + rainfall + melted
    evaporation = (
        (0.3 * solar_incoming_flux + 0.2 * deficit * (1.0 + 0.1 * lowlevel_breeze_rate))
        * wetted
        / (wetted + 2.0)
    )
    remaining = wetted - evaporation
    recharge = 0.4 * jnp.maximum(remaining - 6.0, 0.0)
    return (snowpack, remaining - recharge, saturated + recharge)


def keep_fraction(weights):
    summed = weights[0]
    for direction in range(1, weights.shape[0]):
        summed = summed + weights[direction]
    return 1.0 - summed


def push_sweeps(storage, release_rate, weights, retained):
    rows_here, cols_here = storage.shape
    drained = jnp.zeros_like(storage)
    for sweep_index in range(SWEEPS):
        outflow = release_rate * storage
        fluxes = padded_2(for_sending(weights * outflow[None]), (("row", 1), ("col", 2)), 1)
        inflow = jnp.zeros_like(storage)
        for direction, (down_row, down_col) in enumerate(OFFSETS):
            inflow = (
                inflow
                + fluxes[
                    direction,
                    1 - down_row : 1 - down_row + rows_here,
                    1 - down_col : 1 - down_col + cols_here,
                ]
            )
        storage = storage - outflow + inflow
        drained = drained + retained * outflow
    return (storage, drained)


def lateral_inflow(drained, cell_segment, blocks):
    drain_blocks = drained.reshape(blocks, -1)
    segment_blocks = cell_segment.reshape(blocks, -1)
    labels = jnp.arange(SEG, dtype=jnp.int32)

    def one_block(block_pair):
        values, labels_here = block_pair
        onehot = (labels_here[None, :] == labels[:, None]).astype(jnp.float32)
        return jnp.dot(onehot, values, precision=precise)

    return 0.001 * lax.map(one_block, (drain_blocks, segment_blocks))


def route_blocks(inverse, transfer, drains_into, lateral, entering):
    blocks = inverse.shape[0]
    seg_width = inverse.shape[1]
    carried = jnp.zeros((blocks + 1, seg_width), jnp.float32).at[0].set(entering)
    block_flows = jnp.zeros((blocks, seg_width), jnp.float32)

    def advance(current, carry_state):
        carried, block_flows = carry_state
        source = lateral[current] + carried[current]
        outflow = jnp.dot(inverse[current], source, precision=precise)
        target = drains_into[current]
        carried = carried.at[target].add(transfer[current] * outflow)
        block_flows = block_flows.at[current].set(outflow)
        return (carried, block_flows)

    carried, block_flows = lax.fori_loop(0, blocks, advance, (carried, block_flows))
    return (block_flows, carried[blocks])


def per_device(
    wrf_forcing,
    ground_height_km,
    reflected_share,
    snow_water,
    soil_water,
    saturated,
    release_rate,
    mfd_weights,
    cell_segment,
    route_inverse,
    transfer,
    downstream,
):
    rows_here, cols_here = ground_height_km.shape
    coarse_rows = rows_here // FAC
    coarse_cols = cols_here // FAC
    group_rows = lax.all_gather(wrf_forcing, "col", axis=1, tiled=True)
    rimmed = padded_2(group_rows, (("row", 1),), 1)
    rimmed = extend_rows(rimmed)
    extended = jnp.pad(rimmed, ((0, 0), (0, 0), (1, 1)), mode="edge")
    anchor = (jnp.int32(0), jnp.int32(0), lax.axis_index("col") * coarse_cols)
    padded = lax.dynamic_slice(
        extended, anchor, (extended.shape[0], extended.shape[1], coarse_cols + 2)
    )
    meteorological_drivers = downscale(
        padded, interp_matrix(rows_here, coarse_rows), interp_matrix(cols_here, coarse_cols)
    )
    snowpack, soil_moisture, storage = energy_balance(
        meteorological_drivers, ground_height_km, reflected_share, snow_water, soil_water, saturated
    )
    weights = mfd_weights.astype(jnp.float32)
    groundwater, drained = push_sweeps(storage, release_rate, weights, keep_fraction(weights))
    lateral = lateral_inflow(drained, cell_segment, route_inverse.shape[0])
    drains_into = downstream[:, 0]
    seg_width = route_inverse.shape[1]
    nothing_in = jnp.zeros((seg_width,), jnp.float32)
    col_count = lax.axis_size("col")

    def relay(relay_turn, entering):
        flows_now, leaving = route_blocks(route_inverse, transfer, drains_into, lateral, entering)
        return passed_along(leaving, "col", 1)

    entering = lax.fori_loop(0, col_count - 1, relay, nothing_in)
    channel_flow, leaving = route_blocks(route_inverse, transfer, drains_into, lateral, entering)
    return (snowpack, soil_moisture, groundwater, channel_flow)


def solution(mesh):
    placed = (
        P(None, ("row", "col"), None),
        P("row", "col"),
        P("row", "col"),
        P("row", "col"),
        P("row", "col"),
        P("row", "col"),
        P("row", "col"),
        P(None, "row", "col"),
        P("row", "col"),
        P("row", "col", None),
        P("row", "col"),
        P("row", "col"),
    )
    return jax.shard_map(
        per_device,
        mesh=mesh,
        in_specs=placed,
        out_specs=(P("row", "col"), P("row", "col"), P("row", "col"), P("row", "col")),
        check_vma=False,
    )
```

profile of v0, /device:TPU:40, one launch (start us, length us, event | category | flops | bytes accessed | tf_op | source)
XLA Modules:
  0.0 1649.9 jit_solution(170012153020586962)
XLA Ops:
  1.5 23.6 %all_gather.3 = f32[7,16,256]{2,0,1:T(8,128)S(1)} all-gather(f32[7,1,256]{2,0,1:T(8,128)S(1)} %copy.16), channel_id=1, replica_groups=mesh['row'=8,'col'=16] {'col'}, dimensions={1}, use_global_device_ids=true | all-gather | bytes 121856 | tf_op jit(solution)/shard_map/all_gather | solution.py:177
  27.1 3.6 collective-permute-start.2
  35.9 3.9 collective-permute-start.3
  46.0 4.6 collective-permute-start.5
  54.9 4.6 collective-permute-done.6
  65.5 3.4 collective-permute-start.8
  76.3 3.9 collective-permute-start.10
  100.7 3.9 collective-permute-start.14
  125.4 3.9 collective-permute-start.18
  149.9 3.9 collective-permute-start.22
  174.5 3.9 collective-permute-start.26
  196.5 4.0 collective-permute-start.29
  210.6 3.6 fusion.38
  215.3 32.1 %while.68 = (s32[]{:T(128)}, f32[16,128]{1,0:T(8,128)S(1)}, s32[16,4096]{1,0:T(8,128)}, f32[16,4096]{1,0:T(8,128)S(1)}, s32[]{:T(128)}, /*index=5*/s32[]{:T(128)}) while((s32[]{:T(128)}, f32[16,128]{1,0:T(8,128)S(1)}, s32[16,4096]{1,0:T(8,128)}, f32[16,4096]{1,0:T(8,128)S(1)}, s32[]{:T(128)}, /*index=5*/s32[]{:T(128)}) %tuple.179), condition=%wide.region_1.2_spmd.clone, body=%wide.region_0.1_spmd.clone.sunk | while | flops 6815746 | bytes 67153 | solution.py:138
  249.9 3.4 collective-permute-start.32
  253.3 1294.5 %while.66 = (s32[]{:T(128)}, f32[128]{0:T(128)S(1)}, s32[16]{0:T(128)S(1)}, f32[16,128]{1,0:T(8,128)}, f32[16,128,128]{2,1,0:T(8,128)}, /*index=5*/f32[16,128]{1...) while((s32[]{:T(128)}, f32[128]{0:T(128)S(1)}, ...), condition=%wide.region_6.7_spmd, body=%wide.region_2.6_spmd.sunk | while | flops 197136 | bytes 84433 | solution.py:203
  253.3 78.7 %while.69 = (s32[]{:T(128)}, f32[17,128]{1,0:T(8,128)S(1)}, s32[16]{0:T(128)S(1)}, f32[16,128]{1,0:T(8,128)}, f32[16,128,128]{2,1,0:T(8,128)}, /*index=5*/f32[16...) while((s32[]{:T(128)}, f32[17,128]{1,0:T(8,128)S(1)}, ...), condition=%wide.region_5.5_spmd, body=%wide.region_3.4_spmd.sunk | while | flops 197134 | bytes 71856 | solution.py:156
  334.0 5.6 collective-permute-done
  339.6 78.7 %while.69 = (s32[]{:T(128)}, f32[17,128]{1,0:T(8,128)S(1)}, s32[16]{0:T(128)S(1)}, f32[16,128]{1,0:T(8,128)}, f32[16,128,128]{2,1,0:T(8,128)}, /*index=5*/f32[16...) while((s32[]{:T(128)}, f32[17,128]{1,0:T(8,128)S(1)}, ...), condition=%wide.region_5.5_spmd, body=%wide.region_3.4_spmd.sunk | while | flops 197134 | bytes 71856 | solution.py:156
  420.3 5.6 collective-permute-done
  425.9 78.7 %while.69 = (s32[]{:T(128)}, f32[17,128]{1,0:T(8,128)S(1)}, s32[16]{0:T(128)S(1)}, f32[16,128]{1,0:T(8,128)}, f32[16,128,128]{2,1,0:T(8,128)}, /*index=5*/f32[16...) while((s32[]{:T(128)}, f32[17,128]{1,0:T(8,128)S(1)}, ...), condition=%wide.region_5.5_spmd, body=%wide.region_3.4_spmd.sunk | while | flops 197134 | bytes 71856 | solution.py:156
  506.6 5.6 collective-permute-done
  512.2 78.7 %while.69 = (s32[]{:T(128)}, f32[17,128]{1,0:T(8,128)S(1)}, s32[16]{0:T(128)S(1)}, f32[16,128]{1,0:T(8,128)}, f32[16,128,128]{2,1,0:T(8,128)}, /*index=5*/f32[16...) while((s32[]{:T(128)}, f32[17,128]{1,0:T(8,128)S(1)}, ...), condition=%wide.region_5.5_spmd, body=%wide.region_3.4_spmd.sunk | while | flops 197134 | bytes 71856 | solution.py:156
  592.9 5.6 collective-permute-done
  598.5 78.7 %while.69 = (s32[]{:T(128)}, f32[17,128]{1,0:T(8,128)S(1)}, s32[16]{0:T(128)S(1)}, f32[16,128]{1,0:T(8,128)}, f32[16,128,128]{2,1,0:T(8,128)}, /*index=5*/f32[16...) while((s32[]{:T(128)}, f32[17,128]{1,0:T(8,128)S(1)}, ...), condition=%wide.region_5.5_spmd, body=%wide.region_3.4_spmd.sunk | while | flops 197134 | bytes 71856 | solution.py:156
  679.2 5.6 collective-permute-done
  684.8 78.7 %while.69 = (s32[]{:T(128)}, f32[17,128]{1,0:T(8,128)S(1)}, s32[16]{0:T(128)S(1)}, f32[16,128]{1,0:T(8,128)}, f32[16,128,128]{2,1,0:T(8,128)}, /*index=5*/f32[16...) while((s32[]{:T(128)}, f32[17,128]{1,0:T(8,128)S(1)}, ...), condition=%wide.region_5.5_spmd, body=%wide.region_3.4_spmd.sunk | while | flops 197134 | bytes 71856 | solution.py:156
  765.5 5.6 collective-permute-done
  771.1 78.7 %while.69 = (s32[]{:T(128)}, f32[17,128]{1,0:T(8,128)S(1)}, s32[16]{0:T(128)S(1)}, f32[16,128]{1,0:T(8,128)}, f32[16,128,128]{2,1,0:T(8,128)}, /*index=5*/f32[16...) while((s32[]{:T(128)}, f32[17,128]{1,0:T(8,128)S(1)}, ...), condition=%wide.region_5.5_spmd, body=%wide.region_3.4_spmd.sunk | while | flops 197134 | bytes 71856 | solution.py:156
  851.8 5.6 collective-permute-done
  857.4 78.7 %while.69 = (s32[]{:T(128)}, f32[17,128]{1,0:T(8,128)S(1)}, s32[16]{0:T(128)S(1)}, f32[16,128]{1,0:T(8,128)}, f32[16,128,128]{2,1,0:T(8,128)}, /*index=5*/f32[16...) while((s32[]{:T(128)}, f32[17,128]{1,0:T(8,128)S(1)}, ...), condition=%wide.region_5.5_spmd, body=%wide.region_3.4_spmd.sunk | while | flops 197134 | bytes 71856 | solution.py:156
  938.1 5.6 collective-permute-done
  943.7 78.7 %while.69 = (s32[]{:T(128)}, f32[17,128]{1,0:T(8,128)S(1)}, s32[16]{0:T(128)S(1)}, f32[16,128]{1,0:T(8,128)}, f32[16,128,128]{2,1,0:T(8,128)}, /*index=5*/f32[16...) while((s32[]{:T(128)}, f32[17,128]{1,0:T(8,128)S(1)}, ...), condition=%wide.region_5.5_spmd, body=%wide.region_3.4_spmd.sunk | while | flops 197134 | bytes 71856 | solution.py:156
  1024.4 5.6 collective-permute-done
  1030.0 78.7 %while.69 = (s32[]{:T(128)}, f32[17,128]{1,0:T(8,128)S(1)}, s32[16]{0:T(128)S(1)}, f32[16,128]{1,0:T(8,128)}, f32[16,128,128]{2,1,0:T(8,128)}, /*index=5*/f32[16...) while((s32[]{:T(128)}, f32[17,128]{1,0:T(8,128)S(1)}, ...), condition=%wide.region_5.5_spmd, body=%wide.region_3.4_spmd.sunk | while | flops 197134 | bytes 71856 | solution.py:156
  1110.7 5.6 collective-permute-done
  1116.3 78.7 %while.69 = (s32[]{:T(128)}, f32[17,128]{1,0:T(8,128)S(1)}, s32[16]{0:T(128)S(1)}, f32[16,128]{1,0:T(8,128)}, f32[16,128,128]{2,1,0:T(8,128)}, /*index=5*/f32[16...) while((s32[]{:T(128)}, f32[17,128]{1,0:T(8,128)S(1)}, ...), condition=%wide.region_5.5_spmd, body=%wide.region_3.4_spmd.sunk | while | flops 197134 | bytes 71856 | solution.py:156
  1197.0 5.6 collective-permute-done
  1202.6 78.7 %while.69 = (s32[]{:T(128)}, f32[17,128]{1,0:T(8,128)S(1)}, s32[16]{0:T(128)S(1)}, f32[16,128]{1,0:T(8,128)}, f32[16,128,128]{2,1,0:T(8,128)}, /*index=5*/f32[16...) while((s32[]{:T(128)}, f32[17,128]{1,0:T(8,128)S(1)}, ...), condition=%wide.region_5.5_spmd, body=%wide.region_3.4_spmd.sunk | while | flops 197134 | bytes 71856 | solution.py:156
  1283.3 5.6 collective-permute-done
  1288.9 78.7 %while.69 = (s32[]{:T(128)}, f32[17,128]{1,0:T(8,128)S(1)}, s32[16]{0:T(128)S(1)}, f32[16,128]{1,0:T(8,128)}, f32[16,128,128]{2,1,0:T(8,128)}, /*index=5*/f32[16...) while((s32[]{:T(128)}, f32[17,128]{1,0:T(8,128)S(1)}, ...), condition=%wide.region_5.5_spmd, body=%wide.region_3.4_spmd.sunk | while | flops 197134 | bytes 71856 | solution.py:156
  1369.6 5.6 collective-permute-done
  1375.2 78.7 %while.69 = (s32[]{:T(128)}, f32[17,128]{1,0:T(8,128)S(1)}, s32[16]{0:T(128)S(1)}, f32[16,128]{1,0:T(8,128)}, f32[16,128,128]{2,1,0:T(8,128)}, /*index=5*/f32[16...) while((s32[]{:T(128)}, f32[17,128]{1,0:T(8,128)S(1)}, ...), condition=%wide.region_5.5_spmd, body=%wide.region_3.4_spmd.sunk | while | flops 197134 | bytes 71856 | solution.py:156
  1455.9 5.6 collective-permute-done
  1461.5 78.7 %while.69 = (s32[]{:T(128)}, f32[17,128]{1,0:T(8,128)S(1)}, s32[16]{0:T(128)S(1)}, f32[16,128]{1,0:T(8,128)}, f32[16,128,128]{2,1,0:T(8,128)}, /*index=5*/f32[16...) while((s32[]{:T(128)}, f32[17,128]{1,0:T(8,128)S(1)}, ...), condition=%wide.region_5.5_spmd, body=%wide.region_3.4_spmd.sunk | while | flops 197134 | bytes 71856 | solution.py:156
  1542.2 5.6 collective-permute-done
  1552.8 3.9 collective-permute-start.34
  1556.7 91.1 %while.67 = (s32[]{:T(128)}, f32[17,128]{1,0:T(8,128)S(1)}, f32[16,128]{1,0:T(8,128)S(1)}, s32[16]{0:T(128)S(1)}, f32[16,128]{1,0:T(8,128)}, /*index=5*/f32[16,1...) while((s32[]{:T(128)}, f32[17,128]{1,0:T(8,128)S(1)}, ...), condition=%wide.region_10.11_spmd, body=%wide.region_7.10_spmd.sunk | while | flops 197271 | bytes 74449 | solution.py:156
  (1324 shorter events, 997.7 us)
Async XLA Ops:
  25.1 5.6 collective-permute-start.1
  27.1 5.0 collective-permute-start.2
  35.9 5.8 collective-permute-start.3
  46.0 7.9 collective-permute-start.5
  51.9 7.6 collective-permute-start.6
  63.2 5.6 collective-permute-start.7
  65.5 4.7 collective-permute-start.8
  73.0 7.2 collective-permute-start.9
  76.3 7.6 collective-permute-start.10
  87.6 5.6 collective-permute-start.11
  90.1 4.4 collective-permute-start.12
  97.4 7.2 collective-permute-start.13
  100.7 7.6 collective-permute-start.14
  112.2 5.6 collective-permute-start.15
  114.7 4.4 collective-permute-start.16
  121.9 7.4 collective-permute-start.17
  125.4 7.6 collective-permute-start.18
  136.9 5.6 collective-permute-start.19
  139.4 4.4 collective-permute-start.20
  146.7 7.2 collective-permute-start.21
  149.9 7.6 collective-permute-start.22
  161.5 5.6 collective-permute-start.23
  164.0 4.4 collective-permute-start.24
  171.3 10.4 collective-permute-start.25
  174.5 8.2 collective-permute-start.26
  186.7 6.4 collective-permute-start.27
  189.8 3.8 collective-permute-start.28
  196.5 9.0 collective-permute-start.29
  201.9 7.6 collective-permute-start.30
  247.7 1300.1 %collective-permute-start.31 = (bf16[8,1,256]{2,1,0:T(2,128)(2,1)S(1)}, bf16[8,1,256]{2,1,0:T(2,128)(2,1)S(1)}, u32[]{:S(2)}, u32[]{:S(2)}) collective-permute-start(bf16[8,1,256]{2,1,0:T(2,128)(2,1)S(1)} %get-tuple-element.561), channel_id=1, source_target_pairs={{0,16},{16,32},{32,48},{48,64},{64,80},{80,96},{96,112},{1,17},{17... | collective-permute-start | bytes 12296 | tf_op jit(solution)/shard_map/ppermute | solution.py:27
  249.9 1297.9 %collective-permute-start.32 = (bf16[8,1,256]{2,1,0:T(2,128)(2,1)S(1)}, bf16[8,1,256]{2,1,0:T(2,128)(2,1)S(1)}, u32[]{:S(2)}, u32[]{:S(2)}) collective-permute-start(bf16[8,1,256]{2,1,0:T(2,128)(2,1)S(1)} %get-tuple-element.562), channel_id=1, source_target_pairs={{16,0},{32,16},{48,32},{64,48},{80,64},{96,80},{112,96},{17,1},{33... | collective-permute-start | bytes 12296 | tf_op jit(solution)/shard_map/ppermute | solution.py:29
  332.0 7.6 collective-permute-start
  418.3 7.6 collective-permute-start
  504.6 7.6 collective-permute-start
  590.9 7.6 collective-permute-start
  677.2 7.6 collective-permute-start
  763.5 7.6 collective-permute-start
  849.8 7.6 collective-permute-start
  936.1 7.6 collective-permute-start
  1022.4 7.6 collective-permute-start
  1108.7 7.6 collective-permute-start
  1195.0 7.6 collective-permute-start
  1281.3 7.6 collective-permute-start
  1367.6 7.6 collective-permute-start
  1453.9 7.6 collective-permute-start
  1540.2 7.6 collective-permute-start
  1550.5 97.3 %collective-permute-start.33 = (bf16[8,258,1]{1,0,2:T(8,128)(2,1)S(1)}, bf16[8,258,1]{1,0,2:T(8,128)(2,1)S(1)}, u32[]{:S(2)}, u32[]{:S(2)}) collective-permute-start(bf16[8,258,1]{1,0,2:T(8,128)(2,1)S(1)} %copy.45), channel_id=1, source_target_pairs={{1,0},{2,1},{3,2},{4,3},{5,4},{6,5},{7,6},{8,7},{9,8},{10,9},{11,1... | collective-permute-start | bytes 12392 | tf_op jit(solution)/shard_map/ppermute | solution.py:29
  1552.8 95.4 %collective-permute-start.34 = (bf16[8,258,1]{1,0,2:T(8,128)(2,1)S(1)}, bf16[8,258,1]{1,0,2:T(8,128)(2,1)S(1)}, u32[]{:S(2)}, u32[]{:S(2)}) collective-permute-start(bf16[8,258,1]{1,0,2:T(8,128)(2,1)S(1)} %copy.47), channel_id=1, source_target_pairs={{0,1},{1,2},{2,3},{3,4},{4,5},{5,6},{6,7},{7,8},{8,9},{9,10},{10,1... | collective-permute-start | bytes 12392 | tf_op jit(solution)/shard_map/ppermute | solution.py:27
  (22 other events, 510.8 us)
where the time goes:
time: 1670 us; the launch traced here: 1650 us
  loops' own time  488 us (29%)
  matrix products  451 us (27%)
  local copies, waits for them, and re-layouts  233 us (14%)
  other arithmetic  214 us (13%)
  starting transfers between devices  127 us (8%)
  waiting for transfers between devices  112 us (7%)
  blocking collectives  23.6 us (1%)
    another operation x16, loops' own time, route_blocks(): lax.fori_loop(0, blocks, advance, (carried, block_flows))  487 us
    dot_general x256, matrix products, advance(): outflow = jnp.dot(inverse[current], source, precision=precise)  432 us
    another operation x256, other arithmetic  185 us
    dynamic_slice x256, local copies, waits for them, and re-layouts, advance(): target = drains_into[current]  153 us
    ppermute x15, waiting for transfers between devices, passed_along(): return lax.ppermute(value, axis, pairs)  84.6 us
    ppermute x17, starting transfers between devices, padded_2(): lax.ppermute(tail, axis, [(i, (i + 1) % count) for i in range(ends)])  50.7 us
    ppermute x17, starting transfers between devices, padded_2(): lax.ppermute(head, axis, [((i + 1) % count, i) for i in range(ends)])  47.3 us
  transfers between devices with their start and end apart: 49, of which 29 were waited for; matrix products, arithmetic and copies ran while one was open for 49% of the time, Pallas kernels for 0%

commit v1 on v0

v1 whole, which is shorter than its diff:
```python
import functools

import jax
import jax.numpy as jnp
from jax import lax
from jax.experimental import pallas as pl
from jax.experimental.pallas import tpu as pltpu
from jax.sharding import PartitionSpec as P

MESH = pl.DeviceIdType.MESH
F32, BF16 = jnp.float32, jnp.bfloat16

FAC = 16
VARS = 7
SEG = 128
SWEEPS = 8
NBLK = 16
BR = 16
TILE = 256
RIM = 8
TOP = 16
ROWS = TILE + 32
OFFSETS = ((-1, -1), (-1, 0), (-1, 1), (0, -1), (0, 1), (1, -1), (1, 0), (1, 1))
GROUND, REFLECTED, SNOW, SOIL, STORE, RATE, WEIGHT = range(7)
ARRAYS = 14


def split(x):
    high = x.astype(BF16)
    return high, (x - high.astype(F32)).astype(BF16)


def nn(a, b):
    return lax.dot_general(a, b, (((1,), (0,)), ((), ())), preferred_element_type=F32)


def nt(a, b):
    return lax.dot_general(a, b, (((1,), (1,)), ((), ())), preferred_element_type=F32)


def product(dot, a, b_high, b_low):
    a_high, a_low = split(a)
    return dot(a_high, b_high) + (dot(a_low, b_high) + dot(a_high, b_low))


def iota(shape, dim):
    return lax.broadcasted_iota(jnp.int32, shape, dim)


def kernel(
    n_row,
    n_col,
    forcing,
    ground,
    reflected,
    snow_water,
    soil_water,
    saturated,
    release,
    mfd,
    segment,
    route,
    transfer,
    downstream,
    snow_out,
    soil_out,
    ground_out,
    flow_out,
    ext,
    wb,
    seg,
    inv,
    wmat,
    fmat,
    mats,
    tmat,
    ahot,
    bhot,
    hot,
    strips,
    rims,
    mine,
    rows_in,
    coarse,
    outflow,
    drained,
    retained,
    trans,
    lat,
    flow0,
    gsend,
    gin,
    load_sem,
    store_sem,
    fsend,
    frecv,
    ssend,
    srecv,
    rsend,
    rrecv,
    msend,
    mrecv,
    gsend_sem,
    grecv,
):
    r, c = lax.axis_index("row"), lax.axis_index("col")
    has_up, has_down = r > 0, r < n_row - 1
    has_left, has_right = c > 0, c < n_col - 1

    barrier = pltpu.get_barrier_semaphore()

    def greet(row, col):
        pl.semaphore_signal(barrier, inc=1, device_id=(row, col), device_id_type=MESH)

    @pl.loop(1, n_col)
    def _(d):
        greet(r, lax.rem(c + d, n_col))

    @pl.when(has_up)
    def _():
        greet(r - 1, c)
        greet(r - 1, n_col - 1)

    @pl.when(has_down)
    def _():
        greet(r + 1, c)
        greet(r + 1, 0)

    loads = [pltpu.make_async_copy(route, inv, load_sem.at[0])]
    loads.append(pltpu.make_async_copy(mfd, wb, load_sem.at[1]))
    n = 2
    for k, ref in enumerate((ground, reflected, snow_water, soil_water, saturated, release)):
        for t in range(2):
            loads.append(
                pltpu.make_async_copy(
                    ref.at[:, pl.ds(128 * t, 128)],
                    ext.at[k, t, pl.ds(TOP, TILE), :],
                    load_sem.at[n],
                )
            )
            n += 1
    for t in range(2):
        loads.append(
            pltpu.make_async_copy(segment.at[:, pl.ds(128 * t, 128)], seg.at[t], load_sem.at[n + t])
        )
    for copy in loads[1:]:
        copy.start()
    loads[0].start()

    eye = (iota((SEG, SEG), 0) == iota((SEG, SEG), 1)).astype(F32)
    wmat[NBLK] = eye
    fmat[0] = jnp.zeros((SEG, SEG), F32)
    fmat[1] = jnp.zeros((SEG, SEG), F32)
    fmat[2] = eye
    trans[0:3, :] = jnp.ones((3, SEG), F32)
    trans[3 : 3 + NBLK, :] = transfer[...]
    flow0[0:3, :] = jnp.zeros((3, SEG), F32)
    for v in range(VARS):
        mine[v : v + 1, :] = forcing[v]
    mine[VARS : VARS + 1, :] = jnp.zeros((1, mine.shape[1]), F32)
    rows_in[c + 1] = mine[...]

    @pl.when(jnp.logical_not(has_up))
    def _():
        ext[:, :, pl.ds(TOP - RIM, RIM), :] = jnp.zeros((ARRAYS, 3, RIM, 128), F32)

    @pl.when(jnp.logical_not(has_down))
    def _():
        ext[:, :, pl.ds(TOP + TILE, RIM), :] = jnp.zeros((ARRAYS, 3, RIM, 128), F32)

    pl.semaphore_wait(
        barrier,
        n_col
        - 1
        + has_up.astype(jnp.int32)
        + has_down.astype(jnp.int32)
        + jnp.where(jnp.logical_and(c == n_col - 1, has_down), n_col, 0)
        + jnp.where(jnp.logical_and(c == 0, has_up), n_col, 0),
    )

    def forcing_copy(row, col, slot, sem):
        return pltpu.make_async_remote_copy(
            src_ref=mine,
            dst_ref=rows_in.at[slot],
            send_sem=fsend.at[sem],
            recv_sem=frecv.at[slot],
            device_id=(row, col),
            device_id_type=MESH,
        )

    @pl.loop(1, n_col)
    def _(d):
        forcing_copy(r, lax.rem(c + d, n_col), c + 1, d).start()

    sends_down = jnp.logical_and(c == n_col - 1, has_down)
    sends_up = jnp.logical_and(c == 0, has_up)

    @pl.when(sends_down)
    def _():
        @pl.loop(0, n_col)
        def _(d):
            forcing_copy(r + 1, d, 0, n_col + d).start()

    @pl.when(sends_up)
    def _():
        @pl.loop(0, n_col)
        def _(d):
            forcing_copy(r - 1, d, n_col + 1, 2 * n_col + d).start()

    for copy in loads[1:-2]:
        copy.wait()

    step_rows = 32

    @pl.loop(0, TILE // step_rows)
    def _(i):
        here = pl.ds(pl.multiple_of(i * step_rows, step_rows), step_rows)
        there = pl.ds(pl.multiple_of(TOP + i * step_rows, 8), step_rows)
        lane = iota((step_rows, 128), 1)
        left = jnp.zeros((step_rows, 128), F32)
        right = jnp.zeros((step_rows, 128), F32)
        total = [None, None]
        for k in range(ARRAYS):
            pair = []
            for t in range(2):
                if k < WEIGHT:
                    x = ext[k, t, there, :]
                else:
                    x = wb[k - WEIGHT, here, pl.ds(128 * t, 128)].astype(F32)
                    ext[k, t, there, :] = x
                    total[t] = x if total[t] is None else total[t] + x
                pair.append(x)
            place = jnp.logical_and(lane >= 8 * k, lane < 8 * k + 8)
            left = jnp.where(place, pltpu.roll(pair[0], 8 * k, 1) if k else pair[0], left)
            right = jnp.where(place, pltpu.roll(pair[1], (8 * k + 8) % 128, 1), right)
        for t in range(2):
            retained[t, there, :] = 1.0 - total[t]
        strips[0, here, :] = left
        strips[1, here, :] = right

    def strip_copy(side, col):
        return pltpu.make_async_remote_copy(
            src_ref=strips.at[side],
            dst_ref=rims.at[side],
            send_sem=ssend.at[side],
            recv_sem=srecv.at[side],
            device_id=(r, col),
            device_id_type=MESH,
        )

    @pl.when(has_left)
    def _():
        strip_copy(0, c - 1).start()

    @pl.when(has_right)
    def _():
        strip_copy(1, c + 1).start()

    loads[0].wait()

    def drains_here(block, back):
        before = block - back
        drains = downstream[jnp.maximum(before, 0), 0] == block
        first = jnp.logical_and(block == 0, back == 1)
        return jnp.where(before >= 0, drains, first).astype(F32)

    def responses(start, stop):
        @pl.loop(start, stop)
        def _(i):
            b = NBLK - 1 - i
            high, low = split(inv[b])
            later = wmat[downstream[b, 0]] * trans[pl.ds(b + 3, 1), :]
            wmat[b] = product(nn, later, high, low)
            high, low = split(inv[i])
            carried = jnp.zeros((SEG, SEG), F32)
            for back in range(1, 4):
                share = trans[pl.ds(i + 3 - back, 1), :] * drains_here(i, back)
                carried = carried + fmat[i + 3 - back] * share
            fmat[i + 3] = product(nt, carried, high, low)

    responses(0, 8)

    @pl.when(has_right)
    def _():
        strip_copy(0, c + 1).wait_recv()

    @pl.when(has_left)
    def _():
        strip_copy(1, c - 1).wait_recv()

    @pl.loop(0, TILE // step_rows)
    def _(i):
        here = pl.ds(pl.multiple_of(i * step_rows, step_rows), step_rows)
        there = pl.ds(pl.multiple_of(TOP + i * step_rows, 8), step_rows)
        lane = iota((step_rows, 128), 1)
        at_right = jnp.logical_and(lane < RIM, has_right)
        at_left = jnp.logical_and(lane >= 128 - RIM, has_left)
        from_right = rims[0, here, :]
        from_left = rims[1, here, :]
        for k in range(ARRAYS):
            a = pltpu.roll(from_right, (128 - 8 * k) % 128, 1) if k else from_right
            b = pltpu.roll(from_left, (120 - 8 * k) % 128, 1)
            ext[k, 2, there, :] = jnp.where(at_right, a, jnp.where(at_left, b, 0.0))

    def row_copy(side, row):
        source, target = (TOP, TOP + TILE) if side == 0 else (TOP + TILE - RIM, TOP - RIM)
        return pltpu.make_async_remote_copy(
            src_ref=ext.at[:, :, pl.ds(source, RIM), :],
            dst_ref=ext.at[:, :, pl.ds(target, RIM), :],
            send_sem=rsend.at[side],
            recv_sem=rrecv.at[side],
            device_id=(row, c),
            device_id_type=MESH,
        )

    @pl.when(has_up)
    def _():
        row_copy(0, r - 1).start()

    @pl.when(has_down)
    def _():
        row_copy(1, r + 1).start()

    responses(8, NBLK)

    def matrix_copy(col, slot):
        return pltpu.make_async_remote_copy(
            src_ref=wmat.at[0],
            dst_ref=mats.at[slot],
            send_sem=msend.at[col],
            recv_sem=mrecv.at[slot],
            device_id=(r, col),
            device_id_type=MESH,
        )

    @pl.when(has_left)
    def _():
        @pl.loop(c + 1, n_col)
        def _(col):
            matrix_copy(col, c).start()

    for copy in loads[-2:]:
        copy.wait()

    @pl.loop(0, NBLK)
    def _(b):
        target = pl.ds(pl.multiple_of(b * 16, 16), 16)
        low = iota((16, 128), 0)
        for i in range(BR):
            for t in range(2):
                same = jnp.bitwise_and(seg[t, pl.ds(b * BR + i, 1), :], 15) == low
                bhot[i, target, pl.ds(128 * t, 128)] = jnp.where(same, 1.0, 0.0).astype(BF16)

    @pl.loop(1, n_col)
    def _(d):
        forcing_copy(r, c, lax.rem(c + d, n_col) + 1, 0).wait_recv()

    @pl.when(has_up)
    def _():
        forcing_copy(r, c, 0, 0).wait_recv()

    @pl.when(has_down)
    def _():
        forcing_copy(r, c, n_col + 1, 0).wait_recv()

    @pl.when(jnp.logical_not(has_up))
    def _():
        rows_in[0] = rows_in[1]

    @pl.when(jnp.logical_not(has_down))
    def _():
        rows_in[n_col + 1] = rows_in[n_col]

    cells = rows_in.shape[2]
    lanes = iota((cells, 384), 1)
    column = jnp.where(lanes < 320, lanes, lanes - 384) + c * TILE
    numerator = 2 * column + 1 - FAC
    point = lax.shift_right_arithmetic(numerator, 5)
    fraction = (numerator - 2 * FAC * point).astype(F32) * (1.0 / (2 * FAC))
    place = iota((cells, 384), 0)
    first = jnp.clip(point, 0, cells - 1)
    second = jnp.clip(point + 1, 0, cells - 1)
    spread = (
        jnp.where(place == first, 1.0 - fraction, 0.0) + jnp.where(place == second, fraction, 0.0)
    ).astype(BF16)
    points = rows_in[...].reshape((n_col + 2) * 8, cells)
    high, rest = split(points)
    middle, low = split(points - high.astype(F32))
    wide = nn(high, spread) + (nn(middle, spread) + nn(low, spread))
    for t in range(3):
        coarse[t] = wide[:, 128 * t : 128 * t + 128]

    @pl.when(has_up)
    def _():
        row_copy(0, r - 1).wait_send()
        row_copy(1, r - 1).wait_recv()

    @pl.when(has_down)
    def _():
        row_copy(1, r + 1).wait_send()
        row_copy(0, r + 1).wait_recv()

    outflow[0, :, 0 : TOP - RIM, :] = jnp.zeros((3, TOP - RIM, 128), F32)
    outflow[1, :, 0 : TOP - RIM, :] = jnp.zeros((3, TOP - RIM, 128), F32)
    outflow[0, :, TOP + TILE + RIM :, :] = jnp.zeros((3, RIM, 128), F32)
    outflow[1, :, TOP + TILE + RIM :, :] = jnp.zeros((3, RIM, 128), F32)

    @pl.loop(0, TILE // FAC + 1)
    def _(k):
        rows = pl.ds(pl.multiple_of(TOP - RIM + FAC * k, 8), FAC)
        part = (2 * iota((FAC, 128), 0) + 1).astype(F32) * (1.0 / (2 * FAC))
        for t in range(3):
            v = []
            for var in range(VARS):
                above = coarse[t, pl.ds(k * 8 + var, 1), :]
                below = coarse[t, pl.ds(k * 8 + 8 + var, 1), :]
                v.append(above * (1.0 - part) + below * part)
            heat = -10.0 + 20.0 * v[0] + 6.5 * ((0.5 + 2.0 * v[6]) - ext[GROUND, t, rows, :])
            solar = 0.8 * v[1]
            thermal = 0.25 + 0.15 * v[2]
            deficit = 1.5 * v[3]
            breeze = 0.5 + 6.0 * v[4]
            rain = 4.0 * v[5]
            frozen = rain / (1.0 + jnp.exp(heat / 1.5))
            liquid = rain - frozen
            budget = (
                solar * (1.0 - ext[REFLECTED, t, rows, :]) + thermal - 0.3 + 0.02 * breeze * heat
            )
            pack = ext[SNOW, t, rows, :] + frozen
            melted = jnp.minimum(10.8 * jnp.maximum(budget, 0.0), pack)
            wetted = ext[SOIL, t, rows, :] + liquid + melted
            evaporation = (
                (0.3 * solar + 0.2 * deficit * (1.0 + 0.1 * breeze)) * wetted / (wetted + 2.0)
            )
            remaining = wetted - evaporation
            recharge = 0.4 * jnp.maximum(remaining - 6.0, 0.0)
            storage = ext[STORE, t, rows, :] + recharge
            ext[STORE, t, rows, :] = storage
            outflow[0, t, rows, :] = ext[RATE, t, rows, :] * storage
            if t < 2:
                ext[SNOW, t, rows, :] = pack - melted
                ext[SOIL, t, rows, :] = remaining - recharge
                drained[t, rows, :] = jnp.zeros((FAC, 128), F32)

    outs = []
    for k, (index, ref) in enumerate(((SNOW, snow_out), (SOIL, soil_out), (STORE, ground_out))):
        outs.append(
            [
                pltpu.make_async_copy(
                    ext.at[index, t, pl.ds(TOP, TILE), :],
                    ref.at[:, pl.ds(128 * t, 128)],
                    store_sem.at[2 * k + t],
                )
                for t in range(2)
            ]
        )
    for copy in outs[0] + outs[1]:
        copy.start()

    @pl.loop(0, SWEEPS)
    def _(sweep):
        now = lax.rem(sweep, 2)

        @pl.loop(0, (TILE + 2 * RIM) // 16)
        def _(q):
            base = TOP - RIM + 16 * q
            rows = pl.ds(pl.multiple_of(base, 8), 16)
            lane = iota((16, 128), 1)
            sums = {-1: [], 0: [], 1: []}
            middle = []
            for t in range(3):
                parts = {-1: None, 0: None, 1: None}
                for down_row in (-1, 0, 1):
                    at = rows if down_row == 0 else pl.ds(base - down_row, 16)
                    out = outflow[now, t, at, :]
                    if down_row == 0:
                        middle.append(out)
                    for direction, (dr, dc) in enumerate(OFFSETS):
                        if dr == down_row:
                            term = ext[WEIGHT + direction, t, at, :] * out
                            parts[dc] = term if parts[dc] is None else parts[dc] + term
                for dc in (-1, 0, 1):
                    sums[dc].append(parts[dc])
            east = [pltpu.roll(x, 1, 1) for x in sums[1]]
            west = [pltpu.roll(x, 127, 1) for x in sums[-1]]
            for t in range(3):
                inflow = (
                    sums[0][t]
                    + jnp.where(lane == 0, east[(t + 2) % 3], east[t])
                    + jnp.where(lane == 127, west[(t + 1) % 3], west[t])
                )
                storage = (ext[STORE, t, rows, :] - middle[t]) + inflow
                ext[STORE, t, rows, :] = storage
                outflow[1 - now, t, rows, :] = ext[RATE, t, rows, :] * storage
                if t < 2:
                    drained[t, rows, :] = drained[t, rows, :] + retained[t, rows, :] * middle[t]

    for copy in outs[2]:
        copy.start()

    @pl.loop(0, NBLK)
    def _(b):
        target = pl.ds(pl.multiple_of(b * 16, 16), 16)
        top = iota((8, 128), 0)
        for i in range(BR):
            for t in range(2):
                lanes = pl.ds(128 * t, 128)
                label = seg[t, pl.ds(b * BR + i, 1), :]
                value = drained[t, pl.ds(TOP + b * BR + i, 1), :]
                same = lax.shift_right_logical(label, 4) == top
                kept = jnp.where(same, value, 0.0)
                high = kept.astype(BF16).astype(F32)
                both = jnp.concatenate([high, kept - high], axis=0)
                ahot[i, target, lanes] = both.astype(BF16)

    hot[...] = jnp.zeros((2, TILE, 128), F32)

    @pl.loop(0, BR)
    def _(i):
        a = ahot[i]
        for t in range(2):
            hot[t] = hot[t] + nt(a, bhot[i, 128 * t : 128 * t + 128, :])

    lane = iota((8, 128), 1)
    group = lax.shift_right_logical(lane, 4)
    for b in range(NBLK):
        t = b // 8
        x = hot[t, b * 16 : b * 16 + 8, :] + hot[t, b * 16 + 8 : b * 16 + 16, :]
        x = jnp.where(group == b % 8, x, 0.0)
        for shift in (16, 32, 64):
            x = x + pltpu.roll(x, shift, 1)
        x = jnp.where(group == iota((8, 128), 0), x, 0.0)
        lat[b : b + 1, :] = 0.001 * jnp.sum(x, axis=0, keepdims=True)

    def to_row(matrix):
        column = jnp.sum(matrix, axis=1, keepdims=True)
        same = iota((SEG, SEG), 0) == iota((SEG, SEG), 1)
        return jnp.sum(jnp.where(same, column, 0.0), axis=0, keepdims=True)

    def own(b, total):
        return total + wmat[b] * lat[pl.ds(b, 1), :]

    leaving = to_row(lax.fori_loop(0, NBLK, own, jnp.zeros((SEG, SEG), F32)))
    gsend[...] = jnp.broadcast_to(leaving, (8, SEG))

    def leaving_copy(col, slot):
        return pltpu.make_async_remote_copy(
            src_ref=gsend,
            dst_ref=gin.at[slot],
            send_sem=gsend_sem.at[col],
            recv_sem=grecv.at[slot],
            device_id=(r, col),
            device_id_type=MESH,
        )

    @pl.loop(c + 1, n_col)
    def _(col):
        leaving_copy(col, c).start()

    @pl.loop(1, c)
    def _(slot):
        matrix_copy(c, slot).wait_recv()

    tmat[0] = (iota((SEG, SEG), 0) == iota((SEG, SEG), 1)).astype(F32)

    @pl.loop(0, NBLK)
    def _(b):
        high, low = split(mats[jnp.maximum(c - 1 - b, 0)])
        tmat[b + 1] = product(nn, tmat[b], high, low)
        source = lat[pl.ds(b, 1), :]
        for back in range(1, 4):
            share = trans[pl.ds(b + 3 - back, 1), :] * jnp.where(
                b - back >= 0, drains_here(b, back), 0.0
            )
            source = source + share * flow0[pl.ds(b + 3 - back, 1), :]
        flow0[pl.ds(b + 3, 1), :] = to_row(inv[b] * source)

    @pl.loop(0, c)
    def _(slot):
        leaving_copy(c, slot).wait_recv()

    def enter(k, total):
        return total + tmat[k] * gin[c - 1 - k, 0:1, :]

    total = lax.fori_loop(0, c, enter, jnp.zeros((SEG, SEG), F32))
    entering = jnp.sum(total, axis=1, keepdims=True)

    @pl.loop(0, NBLK)
    def _(b):
        extra = jnp.sum(fmat[b + 3] * entering, axis=0, keepdims=True)
        flow_out[pl.ds(b, 1), :] = flow0[pl.ds(b + 3, 1), :] + extra

    for pair in outs:
        for copy in pair:
            copy.wait()

    @pl.loop(1, n_col)
    def _(d):
        forcing_copy(r, c, 0, d).wait_send()

    @pl.when(sends_down)
    def _():
        @pl.loop(0, n_col)
        def _(d):
            forcing_copy(r, c, 0, n_col + d).wait_send()

    @pl.when(sends_up)
    def _():
        @pl.loop(0, n_col)
        def _(d):
            forcing_copy(r, c, 0, 2 * n_col + d).wait_send()

    @pl.when(has_left)
    def _():
        strip_copy(0, c - 1).wait_send()

        @pl.loop(c + 1, n_col)
        def _(col):
            matrix_copy(col, c).wait_send()

    @pl.when(has_right)
    def _():
        strip_copy(1, c + 1).wait_send()

    @pl.loop(c + 1, n_col)
    def _(col):
        leaving_copy(col, c).wait_send()


def per_device(n_row, n_col, forcing, *args):
    cells = forcing.shape[2]
    any_space = pl.BlockSpec(memory_space=pl.ANY)
    vmem = pl.BlockSpec(memory_space=pltpu.VMEM)
    smem = pl.BlockSpec(memory_space=pltpu.SMEM)
    tile = jax.ShapeDtypeStruct((TILE, TILE), F32)
    dma = pltpu.SemaphoreType.DMA
    return pl.pallas_call(
        functools.partial(kernel, n_row, n_col),
        out_shape=(tile, tile, tile, jax.ShapeDtypeStruct((NBLK, SEG), F32)),
        in_specs=[vmem] + [any_space] * 9 + [vmem, smem],
        out_specs=(any_space, any_space, any_space, vmem),
        scratch_shapes=[
            pltpu.VMEM((ARRAYS, 3, ROWS, 128), F32),
            pltpu.VMEM((8, TILE, TILE), BF16),
            pltpu.VMEM((2, TILE, 128), jnp.int32),
            pltpu.VMEM((NBLK, SEG, SEG), F32),
            pltpu.VMEM((NBLK + 1, SEG, SEG), F32),
            pltpu.VMEM((NBLK + 3, SEG, SEG), F32),
            pltpu.VMEM((n_col, SEG, SEG), F32),
            pltpu.VMEM((NBLK + 1, SEG, SEG), F32),
            pltpu.VMEM((BR, TILE, TILE), BF16),
            pltpu.VMEM((BR, TILE, TILE), BF16),
            pltpu.VMEM((2, TILE, 128), F32),
            pltpu.VMEM((2, TILE, 128), F32),
            pltpu.VMEM((2, TILE, 128), F32),
            pltpu.VMEM((8, cells), F32),
            pltpu.VMEM((n_col + 2, 8, cells), F32),
            pltpu.VMEM((3, (n_col + 2) * 8, 128), F32),
            pltpu.VMEM((2, 3, ROWS, 128), F32),
            pltpu.VMEM((2, ROWS, 128), F32),
            pltpu.VMEM((2, ROWS, 128), F32),
            pltpu.VMEM((24, SEG), F32),
            pltpu.VMEM((NBLK, SEG), F32),
            pltpu.VMEM((24, SEG), F32),
            pltpu.VMEM((8, SEG), F32),
            pltpu.VMEM((n_col, 8, SEG), F32),
            dma((16,)),
            dma((6,)),
            dma((3 * n_col,)),
            dma((n_col + 2,)),
            dma((2,)),
            dma((2,)),
            dma((2,)),
            dma((2,)),
            dma((n_col,)),
            dma((n_col,)),
            dma((n_col,)),
            dma((n_col,)),
        ],
        compiler_params=pltpu.CompilerParams(collective_id=0, has_side_effects=True),
        name="hydrology",
    )(forcing, *args)


def solution(mesh):
    n_row, n_col = mesh.shape["row"], mesh.shape["col"]
    tiles = P("row", "col")
    placed = (
        P(None, ("row", "col"), None),
        *(tiles for _ in range(6)),
        P(None, "row", "col"),
        tiles,
        P("row", "col", None),
        tiles,
        tiles,
    )
    return jax.shard_map(
        functools.partial(per_device, n_row, n_col),
        mesh=mesh,
        in_specs=placed,
        out_specs=(tiles, tiles, tiles, tiles),
        check_vma=False,
    )
```

time: 1670 us -> 51.8 us (0.03)
  the two profiles are of different devices: /device:TPU:40 before, /device:TPU:3 now
where the time goes in v1:
time: 51.8 us; the launch traced here: 51.5 us
  Pallas kernels  45.5 us (88%)
  local copies, waits for them, and re-layouts  5.39 us (10%)
  between operations  0.65 us (1%)
    pallas_call x1, Pallas kernels, per_device(): pl.pallas_call(functools.partial(kernel, n_row, n_col), out_shape=(tile,...  45.5 us
    unnamed x11, local copies, waits for them, and re-layouts  5.39 us

profile of v1, /device:TPU:3, one launch (start us, length us, event | category | flops | bytes accessed | tf_op | source)
XLA Modules:
  0.0 51.5 jit_solution(8750918636801968952)
XLA Ops:
  0.6 1.3 %copy.16.downstream = s32[16,1]{1,0:T(8,128)} copy(s32[16,1]{0,1:T(1,128)} %param.23) | data formatting | bytes 128 | tf_op args[11]
  2.0 45.5 %hydrology.1 = (f32[256,256]{1,0:T(8,128)}, f32[256,256]{1,0:T(8,128)}, f32[256,256]{1,0:T(8,128)}, f32[16,128]{1,0:T(8,128)}) custom-call(f32[7,1,256]{2,1,0:T(1,128)} %forcing.1, f32[256,256]{1,0:T(8,128)} %ground.1, f32[256,256]{1,0:T(8,128)} %reflected.1, f32[256,256]{1,0:T(8,128)} %snow_water.1, f32[256,256]{1,0:T(8,128)} %soil_water.1, ...), custom_call_target="tpu_custom_call" | custom-call | tf_op jit(solution)/shard_map/hydrology/pallas_call | solution.py:637
  47.5 0.0 copy-start.1
  47.5 1.7 %copy.21 = f32[256,256]{1,0:T(8,128)} copy(f32[256,256]{1,0:T(8,128)} %get-tuple-element.8) | data formatting | bytes 524288
  49.2 0.0 copy-done.1
  49.2 0.0 copy-start
  49.2 0.7 %copy.22 = f32[256,256]{1,0:T(8,128)} copy(f32[256,256]{1,0:T(8,128)S(1)} %copy-done.1) | data formatting | bytes 524288
  49.9 0.3 copy-done
  50.2 0.0 copy-start.2
  50.2 0.7 %copy.23 = f32[256,256]{1,0:T(8,128)} copy(f32[256,256]{1,0:T(8,128)S(1)} %copy-done) | data formatting | bytes 524288
  50.9 0.0 copy-done.2
  50.9 0.6 %copy.24 = f32[16,128]{1,0:T(8,128)} copy(f32[16,128]{1,0:T(8,128)S(1)} %copy-done.2) | data formatting | bytes 16384
Async XLA Ops:
  47.5 1.7 %copy-start.1 = (f32[256,256]{1,0:T(8,128)S(1)}, f32[256,256]{1,0:T(8,128)}, u32[]{:S(2)}) copy-start(f32[256,256]{1,0:T(8,128)} %get-tuple-element.9) | copy-start | bytes 786436
  49.2 1.0 %copy-start = (f32[256,256]{1,0:T(8,128)S(1)}, f32[256,256]{1,0:T(8,128)}, u32[]{:S(2)}) copy-start(f32[256,256]{1,0:T(8,128)} %get-tuple-element.10) | copy-start | bytes 786436
  50.2 0.7 %copy-start.2 = (f32[16,128]{1,0:T(8,128)S(1)}, f32[16,128]{1,0:T(8,128)}, u32[]{:S(2)}) copy-start(f32[16,128]{1,0:T(8,128)} %get-tuple-element.11) | copy-start | bytes 24580
